TPU v7x, 32 devices: a whole 2x2x4 slice. The times are simulated.
32 devices in a mesh: layer: 2 (over core), latent: 16 (over z, y, x).
Axes of the slice: x: 2, y: 2, z: 4, core: 2. Of those that a mesh axis runs over, the one named last changes fastest.
Arguments:
- activations: bfloat16 [2, 512, 2048], P('layer', 'latent'), may hold values from -15 to 15
- enc_weight: bfloat16 [2, 2048, 16384], P('layer', None, 'latent'), may hold values from -0.09375 to 0.09375
- enc_bias: float32 [16384], P('latent'), may hold values from -3 to 3
- dec_weight: bfloat16 [2, 16384, 2048], P('layer', 'latent'), may hold values from -0.1796875 to 0.1796875
- dec_bias: float32 [2, 2048], P('layer'), may hold values from -3 to 3
- active_mask: int32 [512, 16384], P(None, 'latent'), may hold values 0 or 1
Outputs:
- grad_enc: bfloat16 [2, 2048, 16384], P('layer', None, 'latent')
- grad_dec: bfloat16 [2, 16384, 2048], P('layer', 'latent')
- loss_value: float32 [], replicated
All inputs are finite; a program needn't handle non-finite values. No bound on the sum of `active_mask` on one device may be relied on, other than what follows from the above.
Results may differ from a plain program's by a relative error of at most 0.0065.
Values may be sent and summed in bfloat16 or wider, within the bound.
A program may use at most 128 MiB of HBM per device.

v0:
```python
import jax
import jax.numpy as jnp
from jax import lax
from jax.sharding import PartitionSpec as P

sparsity_weight = 0.4


def per_device(activations, enc_weight, enc_bias, dec_weight, dec_bias, active_mask):
    local_rows = activations[0]
    encoder = enc_weight[0]
    decoder = dec_weight[0]
    token_all = lax.all_gather(local_rows, "latent", axis=0, tiled=True)
    layer_pre = jnp.dot(token_all, encoder, preferred_element_type=jnp.float32)
    dec_float = decoder.astype(jnp.float32)
    row_norm = jnp.sqrt(jnp.sum(dec_float * dec_float, axis=1) + 1e-06)
    preact, norm_sum = lax.psum((layer_pre, row_norm), "layer")
    preact = preact + enc_bias
    gating = active_mask.astype(jnp.float32)
    latent_code = preact * gating
    code_b = latent_code.astype(jnp.bfloat16)
    layer_index = lax.axis_index("layer")
    recon_share = (
        lax.psum_scatter(
            jnp.dot(code_b, decoder, preferred_element_type=jnp.float32),
            "latent",
            scatter_dimension=0,
            tiled=True,
        )
        + dec_bias[0]
    )
    error_share = recon_share - local_rows.astype(jnp.float32)
    square_part = 0.5 * jnp.sum(error_share * error_share)
    error_b = lax.all_gather(error_share.astype(jnp.bfloat16), "latent", axis=0, tiled=True)
    layer_grad = jnp.einsum("td,fd->tf", error_b, decoder, preferred_element_type=jnp.float32)
    code_grad = lax.psum(layer_grad, "layer") + sparsity_weight * norm_sum
    preact_grad = (code_grad * gating).astype(jnp.bfloat16)
    grad_enc = jnp.einsum(
        "td,tf->df", token_all, preact_grad, preferred_element_type=jnp.float32
    ).astype(jnp.bfloat16)
    code_total = jnp.sum(latent_code, axis=0)
    shrink = sparsity_weight * code_total[:, None] * dec_float / row_norm[:, None]
    grad_dec = (
        jnp.einsum("tf,td->fd", code_b, error_b, preferred_element_type=jnp.float32) + shrink
    ).astype(jnp.bfloat16)
    sparse_part = jnp.where(
        layer_index == 0, sparsity_weight * jnp.sum(latent_code * norm_sum), 0.0
    )
    loss_total = lax.psum(square_part + sparse_part, ("layer", "latent"))
    loss_value = loss_total / (active_mask.shape[0] * token_all.shape[1])
    return (grad_enc[None], grad_dec[None], loss_value)


def solution(mesh):
    placed = (
        P("layer", "latent", None),
        P("layer", None, "latent"),
        P("latent"),
        P("layer", "latent", None),
        P("layer", None),
        P(None, "latent"),
    )
    return jax.shard_map(
        per_device,
        mesh=mesh,
        in_specs=placed,
        out_specs=(P("layer", None, "latent"), P("layer", "latent", None), P()),
        check_vma=False,
    )
```

profile of v0, /device:TPU:1, one launch (start us, length us, event | category | flops | bytes accessed | tf_op | source)
XLA Modules:
  0.0 341.6 jit_solution(5819471263152638103)
XLA Ops:
  7.2 0.0 all-gather.6.cloned.1.call-start
  7.2 0.7 all-gather.6.cloned.1.call-update
  7.9 0.0 all-reduce.3.cloned.1.call-start
  7.9 64.3 %all-gather.6.cloned.1.call-done = bf16[1,512,2048]{2,1,0:T(8,128)(2,1)} async-done(((bf16[1,32,2048]{2,1,0:T(8,128)(2,1)}), bf16[1,512,2048]{2,1,0:T(8,128)(2,1)}) %all-gather.6.cloned.1.call-update) | async-done | bytes 2097168 | tf_op jit(solution)/shard_map/all_gather | solution.py:13
  72.3 6.5 %fusion.8 = f32[512,1024]{1,0:T(8,128)} fusion(bf16[1,2048,1024]{2,1,0:T(8,128)(2,1)} %param.7, bf16[1,512,2048]{2,1,0:T(8,128)(2,1)} %all-gather.6.cloned.1.call-done), kind=kOutput, calls=%fused_computation.10 | convolution fusion | flops 2147483648 | bytes 8388608 | tf_op jit(solution)/shard_map/dot_general | solution.py:14
  78.8 0.0 reduce-scatter.2.cloned.1.call-start
  78.9 3.2 fusion
  82.1 3.7 %psum.30 = f32[1024]{0:T(1024)S(1)} all-reduce(f32[1024]{0:T(1024)S(1)} %add_sqrt_fusion), channel_id=1, replica_groups=mesh['layer'=2,'latent'=16] {'layer'}, use_global_device_ids=true, to_apply=%region_4.0 | all-reduce | flops 1024 | bytes 8192 | tf_op jit(solution)/shard_map/psum | solution.py:17
  85.8 14.6 %all-reduce.3.cloned.1.call-done = f32[512,1024]{1,0:T(8,128)} async-done(((f32[512,1024]{1,0:T(8,128)}), f32[512,1024]{1,0:T(8,128)}) %all-reduce.3.cloned.1.call-update) | async-done | bytes 2097168 | tf_op jit(solution)/shard_map/psum | solution.py:17
  100.4 2.9 multiply_reduce_fusion
  103.3 4.4 %fusion.6 = f32[512,2048]{1,0:T(8,128)} fusion(bf16[1,1024,2048]{2,1,0:T(8,128)(2,1)S(1)} %copy-done, bf16[512,1024]{1,0:T(8,128)(2,1)S(1)} %get-tuple-element.8), kind=kOutput, calls=%fused_computation.8 | convolution fusion | flops 2147483648 | bytes 9437184 | tf_op jit(solution)/shard_map/dot_general | solution.py:25
  107.7 0.0 reduce-scatter.2.cloned.1.call-update
  107.7 0.0 all-gather.4.cloned.1.call-start
  107.7 95.2 %reduce-scatter.2.cloned.1.call-done = f32[32,2048]{1,0:T(8,128)} async-done(((f32[512,2048]{1,0:T(8,128)}), f32[32,2048]{1,0:T(8,128)}) %reduce-scatter.2.cloned.1.call-update) | async-done | bytes 262160 | tf_op jit(solution)/shard_map/reduce_scatter | solution.py:24
  203.0 2.3 multiply_reduce_fusion.1
  205.3 0.0 all-gather.4.cloned.1.call-update
  205.3 0.0 all-reduce.5.cloned.1.call-start
  205.3 60.8 %all-gather.4.cloned.1.call-done = bf16[512,2048]{1,0:T(8,128)(2,1)} async-done(((bf16[32,2048]{1,0:T(8,128)(2,1)}), bf16[512,2048]{1,0:T(8,128)(2,1)}) %all-gather.4.cloned.1.call-update) | async-done | bytes 2097168 | tf_op jit(solution)/shard_map/all_gather | solution.py:34
  266.1 6.5 %fusion.4 = f32[512,1024]{1,0:T(8,128)} fusion(bf16[512,2048]{1,0:T(8,128)(2,1)} %all-gather.4.cloned.1.call-done, bf16[1,1024,2048]{2,1,0:T(8,128)(2,1)} %param.9), kind=kOutput, calls=%fused_computation.6 | convolution fusion | flops 2147483648 | bytes 8388608 | tf_op jit(solution)/shard_map/td,fd->tf/dot_general | solution.py:35
  272.6 0.0 all-reduce.5.cloned.1.call-update
  273.9 39.7 %psum.31 = f32[]{:T(128)} all-reduce(f32[]{:T(128)S(6)} %add.62), channel_id=1, replica_groups=mesh['layer'=2,'latent'=16] {'layer','latent'}, use_global_device_ids=true, to_apply=%region_8.9 | all-reduce | flops 1 | bytes 8 | tf_op jit(solution)/shard_map/psum | solution.py:49
  314.3 6.7 %fusion.10 = bf16[1,1024,2048]{2,1,0:T(8,128)(2,1)} fusion(f32[1024]{0:T(1024)S(1)} %add_sqrt_fusion, bf16[1,1024,2048]{2,1,0:T(8,128)(2,1)} %param.9, f32[1024]{0:T(1024)S(1)} %broadcast_multiply_fusion, bf16[512,2048]{1,0:T(8,128)(2,1)} %all-gather.4.cloned.1.call-done, bf16[512,1024]{1,0:T(8,128)(2,1)S(1)} %get-tuple-element.8), kind=kOutput, calls=%fused_computation.13 | convolution fusion | flops 2157969408 | bytes 11542528 | tf_op jit(solution)/shard_map/tf,td->fd/dot_general | solution.py:44
  321.0 6.5 %convert_bitcast_fusion = bf16[1,2048,1024]{1,2,0:T(8,128)(2,1)} fusion(bf16[1,512,2048]{2,1,0:T(8,128)(2,1)} %all-gather.6.cloned.1.call-done, f32[512,1024]{1,0:T(8,128)} %all-reduce.5.cloned.1.call-done, s32[512,1024]{1,0:T(8,128)S(1)} %copy-done.1, f32[1024]{0:T(1024)S(1)} %broadcast_multiply_fusion.1), kind=kOutput, calls=%fused_computation.12 | convolution fusion | flops 2151677952 | bytes 10489856 | tf_op jit(solution)/shard_map/td,tf->df/dot_general | solution.py:38
  327.5 6.4 %copy.9 = bf16[1,2048,1024]{2,1,0:T(8,128)(2,1)} copy(bf16[1,2048,1024]{1,2,0:T(8,128)(2,1)} %convert_bitcast_fusion) | data formatting | bytes 8388608
  (15 shorter events, 0.1 us)
Async XLA Ops:
  7.2 65.1 %all-gather.6.cloned.1.call-start = ((), (), s32[]{:S(2)}) async-start(), calls=%async_computation.5 | async-start | bytes 2228224 | tf_op jit(solution)/shard_map/all_gather | solution.py:13
  7.9 92.5 %all-reduce.3.cloned.1.call-start = ((), (), s32[]{:S(2)}) async-start(), calls=%async_computation.1 | async-start | bytes 4194304 | tf_op jit(solution)/shard_map/psum | solution.py:17
  78.8 21.6 %copy-start.1 = (s32[512,1024]{1,0:T(8,128)S(1)}, s32[512,1024]{1,0:T(8,128)}, u32[]{:S(2)}) copy-start(s32[512,1024]{1,0:T(8,128)} %param.11) | copy-start | bytes 6291460
  78.8 21.6 %copy-start.4 = (f32[1024]{0:T(1024)S(1)}, f32[1024]{0:T(1024)}, u32[]{:S(2)}) copy-start(f32[1024]{0:T(1024)} %param.8) | copy-start | bytes 12292
  78.8 124.2 %reduce-scatter.2.cloned.1.call-start = ((), (), s32[]{:S(2)}) async-start(), calls=%async_computation.2 | async-start | bytes 4456448 | tf_op jit(solution)/shard_map/reduce_scatter | solution.py:24
  100.4 2.9 copy-start
  107.7 95.3 %copy-start.2 = (bf16[1,32,2048]{2,1,0:T(8,128)(2,1)S(1)}, bf16[1,32,2048]{2,1,0:T(8,128)(2,1)}, u32[]{:S(2)}) copy-start(bf16[1,32,2048]{2,1,0:T(8,128)(2,1)} %param.6) | copy-start | bytes 393220
  107.7 95.3 %copy-start.3 = (f32[1,2048]{1,0:T(1,128)S(1)}, f32[1,2048]{1,0:T(1,128)}, u32[]{:S(2)}) copy-start(f32[1,2048]{1,0:T(1,128)} %param.10) | copy-start | bytes 24580
  107.7 158.4 %all-gather.4.cloned.1.call-start = ((), (), s32[]{:S(2)}) async-start(), calls=%async_computation.3 | async-start | bytes 2228224 | tf_op jit(solution)/shard_map/all_gather | solution.py:34
  205.3 115.7 %all-reduce.5.cloned.1.call-start = ((), (), s32[]{:S(2)}) async-start(), calls=%async_computation.4 | async-start | bytes 4194304 | tf_op jit(solution)/shard_map/psum | solution.py:36
Sparse Core Ops, SparseCore 0:
  10.7 61.4 all-gather.5
  78.9 21.4 all-reduce.2
  107.8 95.1 reduce-scatter.1
  206.2 59.8 all-gather.3
  272.7 21.4 all-reduce.4
where the time goes:
time: 343 us; the launch traced here: 342 us
  waiting for transfers between devices  236 us (69%)
  blocking collectives  43.5 us (13%)
  matrix products  30.6 us (9%)
  between operations  16.9 us (5%)
  other arithmetic  8.39 us (2%)
  local copies, waits for them, and re-layouts  6.41 us (2%)
    reduce_scatter x1, waiting for transfers between devices, per_device(): lax.psum_scatter(jnp.dot(code_b, decoder, preferred_element_type=jnp.floa...  95.2 us
    all_gather x1, waiting for transfers between devices, per_device(): token_all = lax.all_gather(local_rows, 'latent', axis=0, tiled=True)  64.3 us
    all_gather x1, waiting for transfers between devices, per_device(): lax.all_gather(error_share.astype(jnp.bfloat16), 'latent', axis=0, tiled=...  60.8 us
    psum x1, blocking collectives, per_device(): loss_total = lax.psum(square_part + sparse_part, ('layer', 'latent'))  39.7 us
    psum x1, waiting for transfers between devices, per_device(): preact, norm_sum = lax.psum((layer_pre, row_norm), 'layer')  14.6 us
  transfers between devices with their start and end apart: 5, of which 4 were waited for; matrix products, arithmetic and copies ran while one was open for 3% of the time, Pallas kernels for 0%

commit v1 on v0

--- a/solution.py
+++ b/solution.py
@@ -1,12 +1,19 @@
+import functools
+
 import jax
 import jax.numpy as jnp
 from jax import lax
+from jax.experimental import pallas as pl
+from jax.experimental.pallas import tpu as pltpu
 from jax.sharding import PartitionSpec as P
 
 sparsity_weight = 0.4
-
-
-def per_device(activations, enc_weight, enc_bias, dec_weight, dec_bias, active_mask):
+MESH = pl.DeviceIdType.MESH
+F32 = jnp.float32
+BF16 = jnp.bfloat16
+
+
+def plain_step(activations, enc_weight, enc_bias, dec_weight, dec_bias, active_mask):
     local_rows = activations[0]
     encoder = enc_weight[0]
     decoder = dec_weight[0]
@@ -51,6 +58,358 @@
     return (grad_enc[None], grad_dec[None], loss_value)
 
 
+def exchange_kernel(n, group, act, enc_hbm, bias, dec_hbm, dbias, mask_hbm,
+                    tok_t_out, code_t_out, err_out, pg_out, coef, loss_out,
+                    enc, dec, mask, tok, tok_t, own, pre_send, pre_recv, code, code_t,
+                    rs_send, rs_recv, err, lg_send, lg_recv, pg,
+                    norm_own, norm_recv, total, loss_send, loss_recv, pair_send, pair_recv,
+                    load_sem, out_sem, ag_s, ag_r, rs_s, rs_r, er_s, er_r, ls_s, ls_r,
+                    pre_s, pre_r, lg_s, lg_r, nm_s, nm_r, pl_s, pl_r):
+    me = lax.axis_index("latent")
+    layer = lax.axis_index("layer")
+    other = 1 - layer
+    rows, width = act.shape
+    tokens, latents = mask.shape
+    span = group * rows
+    groups = n // group
+    mine = me // group
+    spot = lax.rem(me, group)
+
+    def place(step):
+        half = (step + 1) // 2
+        shift = jnp.where(lax.rem(step, 2) == 1, half, groups - half)
+        return lax.rem(mine + shift, groups)
+
+    def peer(index):
+        return place(index // group) * group + lax.rem(spot + lax.rem(index, group), group)
+
+    loads = [
+        pltpu.make_async_copy(hbm, vmem, load_sem.at[i])
+        for i, (hbm, vmem) in enumerate(((dec_hbm, dec), (enc_hbm, enc), (mask_hbm, mask)))
+    ]
+    for load in loads:
+        load.start()
+
+    barrier = pltpu.get_barrier_semaphore()
+
+    def greet(index, carry):
+        pl.semaphore_signal(barrier, inc=1, device_id={"latent": peer(index)}, device_id_type=MESH)
+        return carry
+
+    lax.fori_loop(1, n, greet, 0)
+    pl.semaphore_signal(barrier, inc=1, device_id={"layer": other}, device_id_type=MESH)
+    pl.semaphore_wait(barrier, n)
+
+    def latent_copy(src, dst, send, recv, target):
+        return pltpu.make_async_remote_copy(
+            src_ref=src, dst_ref=dst, send_sem=send, recv_sem=recv,
+            device_id={"latent": target}, device_id_type=MESH)
+
+    def layer_copy(src, dst, send, recv):
+        return pltpu.make_async_remote_copy(
+            src_ref=src, dst_ref=dst, send_sem=send, recv_sem=recv,
+            device_id={"layer": other}, device_id_type=MESH)
+
+    def token_send(target):
+        return latent_copy(act, tok.at[me], ag_s.at[target], ag_r.at[me], target)
+
+    def token_recv(source):
+        return latent_copy(act, tok.at[source], ag_s.at[source], ag_r.at[source], source)
+
+    def each_peer(do):
+        def body(index, carry):
+            do(peer(index))
+            return carry
+        lax.fori_loop(1, n, body, 0)
+
+    each_peer(lambda t: token_send(t).start())
+    tok[me] = act[...]
+
+    loads[0].wait()
+    lanes = 128
+
+    def norm_block(block, carry):
+        at = pl.multiple_of(block * lanes, lanes)
+        piece = dec[pl.ds(at, lanes), :].astype(F32)
+        sums = jnp.sum(piece * piece, axis=1, keepdims=True)
+        norm = jnp.sqrt(sums + 1e-06)
+        norm_own[:, pl.ds(at, lanes)] = jnp.broadcast_to(norm, (lanes, lanes)).T[0:8, :]
+        return carry
+
+    lax.fori_loop(0, latents // lanes, norm_block, 0)
+    norm_copy = layer_copy(norm_own, norm_recv, nm_s, nm_r)
+    norm_copy.start()
+    total[...] = jnp.zeros_like(total)
+    loads[1].wait()
+    loads[2].wait()
+
+    def rows_of(g):
+        return pl.ds(pl.multiple_of(g * span, span), span)
+
+    def pre_copy(g):
+        return layer_copy(pre_send.at[g], pre_recv.at[g], pre_s.at[g], pre_r.at[g])
+
+    def lg_copy(g):
+        return layer_copy(lg_send.at[g], lg_recv.at[g], lg_s.at[g], lg_r.at[g])
+
+    def rs_copy(target):
+        return latent_copy(rs_send.at[target], rs_recv.at[me], rs_s.at[target], rs_r.at[me], target)
+
+    def rs_wait(source):
+        return latent_copy(rs_send.at[source], rs_recv.at[source], rs_s.at[source], rs_r.at[source], source)
+
+    def wait_group(step, make):
+        def body(j, carry):
+            source = peer(step * group + j)
+
+            @pl.when(source != me)
+            def _():
+                make(source).wait_recv()
+            return carry
+        lax.fori_loop(0, group, body, 0)
+
+    tile = min(512, latents)
+    wide = min(512, width)
+
+    def encode(step):
+        g = place(step)
+        wait_group(step, token_recv)
+        left = tok[pl.ds(g * group, group)].reshape(span, width)
+        for c in range(latents // tile):
+            cols = pl.ds(c * tile, tile)
+            part = jnp.dot(left, enc[:, cols], preferred_element_type=F32)
+            own[rows_of(g), cols] = part
+            pre_send[g, :, cols] = part.astype(BF16)
+        pre_copy(g).start()
+        tok_t[:, rows_of(g)] = left.T
+
+    def decode(step):
+        g = place(step)
+        pre_copy(g).wait_recv()
+        here = rows_of(g)
+        for c in range(latents // tile):
+            cols = pl.ds(c * tile, tile)
+            preact = own[here, cols] + pre_recv[g, :, cols].astype(F32) + bias[0:1, cols]
+            latent = preact * mask[here, cols].astype(F32)
+            total[0:1, cols] += jnp.sum(latent, axis=0, keepdims=True)
+            code[:, cols] = latent.astype(BF16)
+        left = code[...]
+        for c in range(width // wide):
+            cols = pl.ds(c * wide, wide)
+            part = jnp.dot(left, dec[:, cols], preferred_element_type=F32).astype(BF16)
+            rs_send[pl.ds(g * group, group), :, cols] = part.reshape(group, rows, wide)
+
+        def send(j, carry):
+            target = peer(step * group + j)
+
+            @pl.when(target != me)
+            def _():
+                rs_copy(target).start()
+            return carry
+
+        lax.fori_loop(0, group, send, 0)
+        code_t[:, here] = left.T
+
+    def forward(step, carry):
+        @pl.when(step < groups)
+        def _():
+            encode(step)
+
+        @pl.when(step > 0)
+        def _():
+            decode(step - 1)
+        return carry
+
+    lax.fori_loop(0, groups + 1, forward, 0)
+
+    outs = [
+        pltpu.make_async_copy(vmem, hbm, out_sem.at[i])
+        for i, (vmem, hbm) in enumerate(
+            ((tok_t, tok_t_out), (code_t, code_t_out), (err, err_out), (pg, pg_out)))
+    ]
+    outs[0].start()
+    outs[1].start()
+
+    norm_copy.wait()
+    norm_sum = norm_own[0:1, :] + norm_recv[0:1, :]
+    sparse = sparsity_weight * jnp.sum(total[0:1, :] * norm_sum)
+    ratio = sparsity_weight * total[0:1, :] / norm_own[0:1, :]
+    coef[...] = jnp.broadcast_to(ratio, (128, latents)).T
+    norm_recv[...] = jnp.broadcast_to(sparsity_weight * norm_sum, norm_recv.shape)
+
+    rs_recv[me] = rs_send[me]
+    each_peer(lambda s: rs_wait(s).wait_recv())
+    squares = jnp.zeros((1, 1), F32)
+    for c in range(width // wide):
+        cols = pl.ds(c * wide, wide)
+        recon = rs_recv[0, :, cols].astype(F32)
+        for s in range(1, n):
+            recon = recon + rs_recv[s, :, cols].astype(F32)
+        error = recon + dbias[0:1, cols] - act[:, cols].astype(F32)
+        squares = squares + jnp.sum(error * error)
+        err[me, :, cols] = error.astype(BF16)
+    partial = 0.5 * squares + jnp.where(layer == 0, sparse, 0.0)
+    loss_send[...] = jnp.broadcast_to(partial, loss_send.shape)
+    loss_recv[me] = loss_send[...]
+
+    def err_send(target):
+        return latent_copy(err.at[me], err.at[me], er_s.at[target], er_r.at[me], target)
+
+    def err_recv(source):
+        return latent_copy(err.at[source], err.at[source], er_s.at[source], er_r.at[source], source)
+
+    def loss_copy(target):
+        return latent_copy(loss_send, loss_recv.at[me], ls_s.at[target], ls_r.at[me], target)
+
+    def loss_wait(source):
+        return latent_copy(loss_send, loss_recv.at[source], ls_s.at[source], ls_r.at[source], source)
+
+    each_peer(lambda t: err_send(t).start())
+    each_peer(lambda t: loss_copy(t).start())
+
+    def grad(step):
+        g = place(step)
+        wait_group(step, err_recv)
+        left = err[pl.ds(g * group, group)].reshape(span, width)
+        for c in range(latents // tile):
+            part = lax.dot_general(
+                left, dec[pl.ds(c * tile, tile), :], (((1,), (1,)), ((), ())),
+                preferred_element_type=F32)
+            cols = pl.ds(c * tile, tile)
+            own[rows_of(g), cols] = part
+            lg_send[g, :, cols] = part.astype(BF16)
+        lg_copy(g).start()
+
+    def gate(step):
+        g = place(step)
+        here = rows_of(g)
+        lg_copy(g).wait_recv()
+        for c in range(latents // tile):
+            cols = pl.ds(c * tile, tile)
+            code_grad = own[here, cols] + lg_recv[g, :, cols].astype(F32) + norm_recv[0:1, cols]
+            pg[here, cols] = (code_grad * mask[here, cols].astype(F32)).astype(BF16)
+
+    def backward(step, carry):
+        @pl.when(step < groups)
+        def _():
+            grad(step)
+
+        @pl.when(step > 0)
+        def _():
+            gate(step - 1)
+        return carry
+
+    lax.fori_loop(0, groups + 1, backward, 0)
+    outs[2].start()
+    outs[3].start()
+
+    each_peer(lambda s: loss_wait(s).wait_recv())
+    pair_send[...] = jnp.sum(loss_recv[...], axis=0)
+    pair = layer_copy(pair_send, pair_recv, pl_s, pl_r)
+    pair.start()
+
+    def finish(target):
+        token_send(target).wait_send()
+        rs_copy(target).wait_send()
+        err_send(target).wait_send()
+        loss_copy(target).wait_send()
+
+    each_peer(finish)
+
+    def finish_pair(g, carry):
+        pre_copy(g).wait_send()
+        lg_copy(g).wait_send()
+        return carry
+
+    lax.fori_loop(0, groups, finish_pair, 0)
+    pair.wait()
+    loss_out[...] = (pair_send[...] + pair_recv[...]) / (tokens * width)
+    for out in outs:
+        out.wait()
+
+
+def grads_kernel(tok_t, pg, code_t, err, dec, coef, enc_out, dec_out):
+    enc_out[...] = jnp.dot(tok_t[...], pg[...], preferred_element_type=F32).astype(BF16)
+    shrink = coef[:, 0:1] * dec[...].astype(F32)
+    dec_out[...] = (jnp.dot(code_t[...], err[...], preferred_element_type=F32) + shrink).astype(BF16)
+
+
+def fast_step(n, activations, enc_weight, enc_bias, dec_weight, dec_bias, active_mask):
+    rows, width = activations.shape[1:]
+    tokens, latents = active_mask.shape
+    group = max(1, min(n, 128 // rows))
+    groups = n // group
+    span = group * rows
+    decoder = dec_weight[0]
+    vmem = pl.BlockSpec(memory_space=pltpu.VMEM)
+    anyw = pl.BlockSpec(memory_space=pl.ANY)
+    shape = jax.ShapeDtypeStruct
+    dma = pltpu.SemaphoreType.DMA
+    tok_t, code_t, err, pg, coef, loss = pl.pallas_call(
+        functools.partial(exchange_kernel, n, group),
+        out_shape=(
+            shape((width, tokens), BF16),
+            shape((latents, tokens), BF16),
+            shape((n, rows, width), BF16),
+            shape((tokens, latents), BF16),
+            shape((latents, 128), F32),
+            shape((8, 128), F32),
+        ),
+        in_specs=[vmem, anyw, vmem, anyw, vmem, anyw],
+        out_specs=(anyw, anyw, anyw, anyw, vmem, vmem),
+        scratch_shapes=[
+            pltpu.VMEM((width, latents), BF16),
+            pltpu.VMEM((latents, width), BF16),
+            pltpu.VMEM((tokens, latents), jnp.int32),
+            pltpu.VMEM((n, rows, width), BF16),
+            pltpu.VMEM((width, tokens), BF16),
+            pltpu.VMEM((tokens, latents), F32),
+            pltpu.VMEM((groups, span, latents), BF16),
+            pltpu.VMEM((groups, span, latents), BF16),
+            pltpu.VMEM((span, latents), BF16),
+            pltpu.VMEM((latents, tokens), BF16),
+            pltpu.VMEM((n, rows, width), BF16),
+            pltpu.VMEM((n, rows, width), BF16),
+            pltpu.VMEM((n, rows, width), BF16),
+            pltpu.VMEM((groups, span, latents), BF16),
+            pltpu.VMEM((groups, span, latents), BF16),
+            pltpu.VMEM((tokens, latents), BF16),
+            pltpu.VMEM((8, latents), F32),
+            pltpu.VMEM((8, latents), F32),
+            pltpu.VMEM((8, latents), F32),
+            pltpu.VMEM((8, 128), F32),
+            pltpu.VMEM((n, 8, 128), F32),
+            pltpu.VMEM((8, 128), F32),
+            pltpu.VMEM((8, 128), F32),
+            dma((3,)), dma((4,)),
+            dma((n,)), dma((n,)), dma((n,)), dma((n,)), dma((n,)), dma((n,)), dma((n,)), dma((n,)),
+            dma((groups,)), dma((groups,)), dma((groups,)), dma((groups,)),
+            dma, dma, dma, dma,
+        ],
+        compiler_params=pltpu.CompilerParams(collective_id=0, has_side_effects=True),
+    )(activations[0], enc_weight[0], enc_bias[None], decoder, dec_bias, active_mask)
+    err = err.reshape(tokens, width)
+    tile = min(256, latents)
+    grad_enc, grad_dec = pl.pallas_call(
+        grads_kernel,
+        grid=(latents // tile,),
+        out_shape=(shape((width, latents), BF16), shape((latents, width), BF16)),
+        in_specs=[
+            pl.BlockSpec((width, tokens), lambda i: (0, 0)),
+            pl.BlockSpec((tokens, tile), lambda i: (0, i)),
+            pl.BlockSpec((tile, tokens), lambda i: (i, 0)),
+            pl.BlockSpec((tokens, width), lambda i: (0, 0)),
+            pl.BlockSpec((tile, width), lambda i: (i, 0)),
+            pl.BlockSpec((tile, 128), lambda i: (i, 0)),
+        ],
+        out_specs=(
+            pl.BlockSpec((width, tile), lambda i: (0, i)),
+            pl.BlockSpec((tile, width), lambda i: (i, 0)),
+        ),
+    )(tok_t, pg, code_t, err, decoder, coef)
+    return (grad_enc[None], grad_dec[None], loss[0, 0])
+
+
 def solution(mesh):
     placed = (
         P("layer", "latent", None),
@@ -60,6 +419,14 @@
         P("layer", None),
         P(None, "latent"),
     )
+    n = mesh.shape["latent"]
+
+    def per_device(activations, *others):
+        rows = activations.shape[1]
+        if rows % 16 == 0 and 128 % rows == 0:
+            return fast_step(n, activations, *others)
+        return plain_step(activations, *others)
+
     return jax.shard_map(
         per_device,
         mesh=mesh,

time: 343 us -> 164 us (0.48)
  waiting for transfers between devices: 236 us -> 0 us
  Pallas kernels: 0 us -> 162 us
  blocking collectives: 43.5 us -> 0 us
  matrix products: 30.6 us -> 0 us
  between operations: 16.9 us -> 0.64 us
  other arithmetic: 8.39 us -> 0 us
  local copies, waits for them, and re-layouts: 6.41 us -> 1.19 us
    pallas_call x0 -> x2, Pallas kernels: none -> 162 us  [the longest x1 151 us: fast_step(): pl.pallas_call(functools.partial(exchange_kernel, n, group), out_shape=(s...]
    all_gather x2 -> x0, waiting for transfers between devices: 125 us -> none  [the longest x1 64.3 us: per_device(): token_all = lax.all_gather(local_rows, 'latent', axis=0, tiled=True)]
    reduce_scatter x1 -> x0, waiting for transfers between devices: 95.2 us -> none  [per_device(): lax.psum_scatter(jnp.dot(code_b, decoder, preferred_element_type=jnp.floa...]
    psum x2 -> x0, blocking collectives: 43.5 us -> none  [the longest x1 39.7 us: per_device(): loss_total = lax.psum(square_part + sparse_part, ('layer', 'latent'))]
    dot_general x5 -> x0, matrix products: 30.6 us -> none  [the longest x1 6.67 us: per_device(): jnp.einsum('tf,td->fd', code_b, error_b, preferred_element_type=jnp.float32)]
    psum x2 -> x0, waiting for transfers between devices: 14.6 us -> none  [the longest x1 14.6 us: per_device(): preact, norm_sum = lax.psum((layer_pre, row_norm), 'layer')]
    reduce_sum x3 -> x0, other arithmetic: 8.37 us -> none  [the longest x1 3.21 us: per_device(): row_norm = jnp.sqrt(jnp.sum(dec_float * dec_float, axis=1) + 1e-06)]
    unnamed x11 -> x0, local copies, waits for them, and re-layouts: 6.41 us -> none
  transfers between devices with their start and end apart: 5 -> 0, of which waited for: 4 -> 0; matrix products, arithmetic and copies ran while one was open for 3% -> 0% of each run, Pallas kernels for 0% -> 0%
where the time goes in v1:
time: 164 us; the launch traced here: 163 us
  Pallas kernels  162 us (99%)
    pallas_call x1, Pallas kernels, fast_step(): pl.pallas_call(functools.partial(exchange_kernel, n, group), out_shape=(s...  151 us
    pallas_call x1, Pallas kernels, fast_step(): pl.pallas_call(grads_kernel, grid=(latents // tile,), out_shape=(shape((w...  10.3 us

profile of v1, /device:TPU:1, one launch (start us, length us, event | category | flops | bytes accessed | tf_op | source)
XLA Modules:
  0.0 163.3 jit_solution(190785462828897549)
XLA Ops:
  0.6 151.2 %shard_map.85 = (bf16[2048,512]{1,0:T(8,128)(2,1)}, bf16[1024,512]{1,0:T(8,128)(2,1)}, bf16[16,32,2048]{2,1,0:T(8,128)(2,1)}, bf16[512,1024]{1,0:T(8,128)(2,1)}, f32[1024,128]{1,0:T(8,128)}, /*index=5*/f32[8,128]{1,0:T(8,128)}) custom-call(bf16[32,2048]{1,0:T(8,128)(2,1)} %bitcast.12, bf16[2048,1024]{1,0:T(8,128)(2,1)} %bitcast.10, f32[1,1024]{1,0:T(1,128)} %bitcast.13, ...), custom_call_target="tpu_custom_call" | custom-call | tf_op jit(solution)/shard_map/pallas_call | solution.py:348
  151.9 1.2 slice.3
  153.0 10.3 %shard_map.86 = (bf16[2048,1024]{1,0:T(8,128)(2,1)}, bf16[1024,2048]{1,0:T(8,128)(2,1)}) custom-call(bf16[2048,512]{1,0:T(8,128)(2,1)} %get-tuple-element.11.tok_t, bf16[512,1024]{1,0:T(8,128)(2,1)} %get-tuple-element.12.pg, bf16[1024,512]{1,0:T(8,128)(2,1)} %get-tuple-element.13.code_t, bf16[512,2048]{1,0:T(8,128)(2,1)} %bitcast.11, ...), custom_call_target="tpu_custom_call" | custom-call | tf_op jit(solution)/shard_map/pallas_call | solution.py:393
